TPU v7x, 32 devices: a whole 2x2x4 slice. The times are simulated.
32 devices in a mesh: rep: 2 (over x), shard: 16 (over z, y, core).
Axes of the slice: x: 2, y: 2, z: 4, core: 2. Of those that a mesh axis runs over, the one named last changes fastest.
Arguments:
- inputs: bfloat16 [32, 1024, 768], P(('rep', 'shard')), may hold values from -6 to 6
- doc_ids: int32 [32, 1024], P(('rep', 'shard')), may hold values from 0 to 3, never falling along the last dimension, each value on 1 to 512 neighbouring positions
- attn_gain: bfloat16 [768], P('shard'), may hold values from 0.25 to 1.75
- w_query: bfloat16 [768, 768], P('shard'), may hold values from -0.21875 to 0.21875
- w_key: bfloat16 [768, 768], P('shard'), may hold values from -0.21875 to 0.21875
- w_value: bfloat16 [768, 768], P('shard'), may hold values from -0.21875 to 0.21875
- w_out: bfloat16 [768, 768], P('shard'), may hold values from -1.75 to 1.75
- ffn_gain: bfloat16 [768], P('shard'), may hold values from 0.25 to 1.75
- w_gate: bfloat16 [768, 2048], P('shard'), may hold values from -0.21875 to 0.21875
- w_up: bfloat16 [768, 2048], P('shard'), may hold values from -0.21875 to 0.21875
- w_down: bfloat16 [2048, 768], P('shard'), may hold values from -0.125 to 0.125
- cotangent: bfloat16 [32, 1024, 768], P(('rep', 'shard')), may hold values from -6 to 6
Outputs:
- output: bfloat16 [32, 1024, 768], P(('rep', 'shard'))
- grad_input: float32 [32, 1024, 768], P(('rep', 'shard'))
- grad_attn_gain: float32 [768], P('shard')
- grad_w_query: float32 [768, 768], P('shard')
- grad_w_key: float32 [768, 768], P('shard')
- grad_w_value: float32 [768, 768], P('shard')
- grad_w_out: float32 [768, 768], P('shard')
- grad_ffn_gain: float32 [768], P('shard')
- grad_w_gate: float32 [768, 2048], P('shard')
- grad_w_up: float32 [768, 2048], P('shard')
- grad_w_down: float32 [2048, 768], P('shard')
Inputs may be any that keep to these rules, and one draw needn't show every extreme that they name: `doc_ids`: within a sequence document numbers never fall; every document has 1 to 512 tokens, and one has exactly 512.
All inputs are finite; a program needn't handle non-finite values.
Results may differ from a plain program's by a relative error of at most 0.017.
Values may be sent and summed in bfloat16 or wider, within the bound.
No kernel may reach another device: no remote copies, remote signals or barrier semaphores. Data moves between devices by JAX's collectives and lax.ppermute only.
A program may use at most 320 MiB of HBM per device.

v0:
```python
import jax
import jax.numpy as jnp
from jax import lax
from jax.sharding import PartitionSpec as P

H = 12
HD = 64
BLOCK = 256
epsilon = 1e-06
rope_base = 10000.0
masked_score = -1e30


def rope_tables(length, head_size):
    position = jnp.arange(length, dtype=jnp.float32)
    exponent = jnp.arange(head_size // 2, dtype=jnp.float32) * (2.0 / head_size)
    angles = position[:, None] * jnp.power(rope_base, -exponent)[None, :]
    return (jnp.cos(angles)[:, None, :], jnp.sin(angles)[:, None, :])


def rotate(tensor, cosine_table, sine_table):
    midway = tensor.shape[-1] // 2
    front_half = tensor[..., :midway]
    back_half = tensor[..., midway:]
    return jnp.concatenate(
        [
            front_half * cosine_table - back_half * sine_table,
            back_half * cosine_table + front_half * sine_table,
        ],
        axis=-1,
    )


def rotate_back(tensor, cosine_table, sine_table):
    midway = tensor.shape[-1] // 2
    front_half = tensor[..., :midway]
    back_half = tensor[..., midway:]
    return jnp.concatenate(
        [
            front_half * cosine_table + back_half * sine_table,
            back_half * cosine_table - front_half * sine_table,
        ],
        axis=-1,
    )


def allowed_pairs(doc_ids, offset, row_step, block_size):
    length = doc_ids.shape[1]
    row_docs = lax.dynamic_slice_in_dim(doc_ids, offset, row_step, 1)
    row_block = (offset + jnp.arange(row_step, dtype=jnp.int32)) // block_size
    col_block = jnp.arange(length, dtype=jnp.int32) // block_size
    same_doc = row_docs[:, :, None] == doc_ids[:, None, :]
    ordered = col_block[None, None, :] <= row_block[None, :, None]
    return (same_doc & ordered)[:, None, :, :]


def rows_product(left, right):
    return lax.dot_general(
        left, right, (((0,), (0,)), ((), ())), preferred_element_type=jnp.float32
    )


def right_transposed(left, right):
    return lax.dot_general(
        left, right, (((1,), (1,)), ((), ())), preferred_element_type=jnp.float32
    )


def norm_back(grad_normed, normed, inverse):
    return inverse * (grad_normed - normed * jnp.mean(grad_normed * normed, -1, keepdims=True))


def block_scores(query_block, keys_rot, doc_ids, offset, row_step, factor):
    allowed = allowed_pairs(doc_ids, offset, row_step, BLOCK)
    scores = (
        jnp.einsum("bqhd,bkhd->bhqk", query_block, keys_rot, preferred_element_type=jnp.float32)
        * factor
    )
    return jnp.where(allowed, scores, masked_score)


def per_device(
    inputs,
    doc_ids,
    attn_gain,
    w_query,
    w_key,
    w_value,
    w_out,
    ffn_gain,
    w_gate,
    w_up,
    w_down,
    cotangent,
):
    batch_size, length, model_width = inputs.shape
    rows_total = batch_size * length
    head_count = H
    head_size = HD
    row_step = min(512, length)
    factor = head_size ** (-0.5)
    gain_one, query_mat, key_mat, value_mat, out_mat, gain_two, gate_mat, up_mat, down_mat = (
        lax.all_gather(attn_gain, "shard", axis=0, tiled=True),
        lax.all_gather(w_query, "shard", axis=0, tiled=True),
        lax.all_gather(w_key, "shard", axis=0, tiled=True),
        lax.all_gather(w_value, "shard", axis=0, tiled=True),
        lax.all_gather(w_out, "shard", axis=0, tiled=True),
        lax.all_gather(ffn_gain, "shard", axis=0, tiled=True),
        lax.all_gather(w_gate, "shard", axis=0, tiled=True),
        lax.all_gather(w_up, "shard", axis=0, tiled=True),
        lax.all_gather(w_down, "shard", axis=0, tiled=True),
    )
    resid = inputs.astype(jnp.float32).reshape(rows_total, model_width)
    inv_one = lax.rsqrt(jnp.mean(resid * resid, -1, keepdims=True) + epsilon)
    normed_one = resid * inv_one
    gain_first = gain_one.astype(jnp.float32)
    attn_in = (normed_one * gain_first).astype(jnp.bfloat16)
    cosine_table, sine_table = rope_tables(length, head_size)

    def project(matrix):
        return jnp.dot(attn_in, matrix, preferred_element_type=jnp.float32).reshape(
            batch_size, length, head_count, head_size
        )

    queries = rotate(project(query_mat), cosine_table, sine_table).astype(jnp.bfloat16)
    keys_rot = rotate(project(key_mat), cosine_table, sine_table).astype(jnp.bfloat16)
    value_vec = project(value_mat).astype(jnp.bfloat16)
    mixed_blocks = []
    log_sums = []
    for offset in range(0, length, row_step):
        query_block = queries[:, offset : offset + row_step]
        scores = block_scores(query_block, keys_rot, doc_ids, offset, row_step, factor)
        row_peak = jnp.max(scores, -1, keepdims=True)
        exp_scores = jnp.exp(scores - row_peak)
        row_total = jnp.sum(exp_scores, -1, keepdims=True)
        attn_probs = (exp_scores / row_total).astype(jnp.bfloat16)
        log_sums.append(row_peak + jnp.log(row_total))
        mixed_blocks.append(
            jnp.einsum("bhqk,bkhd->bqhd", attn_probs, value_vec, preferred_element_type=jnp.float32)
        )
    mixed_heads = (
        jnp.concatenate(mixed_blocks, 1).reshape(rows_total, model_width).astype(jnp.bfloat16)
    )
    middle = resid + jnp.dot(mixed_heads, out_mat, preferred_element_type=jnp.float32)
    inv_two = lax.rsqrt(jnp.mean(middle * middle, -1, keepdims=True) + epsilon)
    normed_two = middle * inv_two
    gain_second = gain_two.astype(jnp.float32)
    ffn_in = (normed_two * gain_second).astype(jnp.bfloat16)
    gate_pre = jnp.dot(ffn_in, gate_mat, preferred_element_type=jnp.float32)
    up_pre = jnp.dot(ffn_in, up_mat, preferred_element_type=jnp.float32)
    gate_sigmoid = jax.nn.sigmoid(gate_pre)
    hidden = (gate_pre * gate_sigmoid * up_pre).astype(jnp.bfloat16)
    result = middle + jnp.dot(hidden, down_mat, preferred_element_type=jnp.float32)
    output = result.astype(jnp.bfloat16).reshape(batch_size, length, model_width)
    gain_one, query_mat, key_mat, value_mat, out_mat, gain_two, gate_mat, up_mat, down_mat = (
        lax.all_gather(attn_gain, "shard", axis=0, tiled=True),
        lax.all_gather(w_query, "shard", axis=0, tiled=True),
        lax.all_gather(w_key, "shard", axis=0, tiled=True),
        lax.all_gather(w_value, "shard", axis=0, tiled=True),
        lax.all_gather(w_out, "shard", axis=0, tiled=True),
        lax.all_gather(ffn_gain, "shard", axis=0, tiled=True),
        lax.all_gather(w_gate, "shard", axis=0, tiled=True),
        lax.all_gather(w_up, "shard", axis=0, tiled=True),
        lax.all_gather(w_down, "shard", axis=0, tiled=True),
    )
    branch_grad = cotangent.reshape(rows_total, model_width)
    grad_out = branch_grad.astype(jnp.float32)
    grad_w_down = rows_product(hidden, branch_grad)
    grad_hidden = right_transposed(branch_grad, down_mat)
    grad_gate = (
        grad_hidden * up_pre * gate_sigmoid * (1.0 + gate_pre * (1.0 - gate_sigmoid))
    ).astype(jnp.bfloat16)
    grad_up = (grad_hidden * gate_pre * gate_sigmoid).astype(jnp.bfloat16)
    grad_w_gate = rows_product(ffn_in, grad_gate)
    grad_w_up = rows_product(ffn_in, grad_up)
    grad_ffn_in = right_transposed(grad_gate, gate_mat) + right_transposed(grad_up, up_mat)
    grad_gain_two = jnp.sum(grad_ffn_in * normed_two, 0)
    grad_middle = grad_out + norm_back(grad_ffn_in * gain_second, normed_two, inv_two)
    attn_grad = grad_middle.astype(jnp.bfloat16)
    grad_w_out = rows_product(mixed_heads, attn_grad)
    grad_mixed = (
        right_transposed(attn_grad, out_mat)
        .astype(jnp.bfloat16)
        .reshape(batch_size, length, head_count, head_size)
    )
    grad_key = jnp.zeros((batch_size, length, head_count, head_size), jnp.float32)
    grad_value = jnp.zeros((batch_size, length, head_count, head_size), jnp.float32)
    grad_query_blocks = []
    for block_index, offset in enumerate(range(0, length, row_step)):
        query_block = queries[:, offset : offset + row_step]
        scores = block_scores(query_block, keys_rot, doc_ids, offset, row_step, factor)
        probs_full = jnp.exp(scores - log_sums[block_index])
        attn_probs = probs_full.astype(jnp.bfloat16)
        grad_block = grad_mixed[:, offset : offset + row_step]
        grad_value = grad_value + jnp.einsum(
            "bhqk,bqhd->bkhd", attn_probs, grad_block, preferred_element_type=jnp.float32
        )
        grad_probs = jnp.einsum(
            "bqhd,bkhd->bhqk", grad_block, value_vec, preferred_element_type=jnp.float32
        )
        grad_scores = (
            probs_full * (grad_probs - jnp.sum(probs_full * grad_probs, -1, keepdims=True))
        ).astype(jnp.bfloat16)
        grad_query_blocks.append(
            jnp.einsum("bhqk,bkhd->bqhd", grad_scores, keys_rot, preferred_element_type=jnp.float32)
            * factor
        )
        grad_key = (
            grad_key
            + jnp.einsum(
                "bhqk,bqhd->bkhd", grad_scores, query_block, preferred_element_type=jnp.float32
            )
            * factor
        )
    grad_query_rot = jnp.concatenate(grad_query_blocks, 1)
    grad_query = (
        rotate_back(grad_query_rot, cosine_table, sine_table)
        .astype(jnp.bfloat16)
        .reshape(rows_total, model_width)
    )
    grad_key_low = (
        rotate_back(grad_key, cosine_table, sine_table)
        .astype(jnp.bfloat16)
        .reshape(rows_total, model_width)
    )
    grad_value_low = grad_value.astype(jnp.bfloat16).reshape(rows_total, model_width)
    grad_w_query = rows_product(attn_in, grad_query)
    grad_w_key = rows_product(attn_in, grad_key_low)
    grad_w_value = rows_product(attn_in, grad_value_low)
    grad_attn_in = (
        right_transposed(grad_query, query_mat)
        + right_transposed(grad_key_low, key_mat)
        + right_transposed(grad_value_low, value_mat)
    )
    grad_gain_one = jnp.sum(grad_attn_in * normed_one, 0)
    grad_input = (grad_middle + norm_back(grad_attn_in * gain_first, normed_one, inv_one)).reshape(
        batch_size, length, model_width
    )
    replicas = lax.axis_size("rep")
    members = lax.axis_size("shard")
    parts = (
        lax.psum_scatter(grad_gain_one, "shard", scatter_dimension=0, tiled=True),
        lax.psum_scatter(grad_w_query, "shard", scatter_dimension=0, tiled=True),
        lax.psum_scatter(grad_w_key, "shard", scatter_dimension=0, tiled=True),
        lax.psum_scatter(grad_w_value, "shard", scatter_dimension=0, tiled=True),
        lax.psum_scatter(grad_w_out, "shard", scatter_dimension=0, tiled=True),
        lax.psum_scatter(grad_gain_two, "shard", scatter_dimension=0, tiled=True),
        lax.psum_scatter(grad_w_gate, "shard", scatter_dimension=0, tiled=True),
        lax.psum_scatter(grad_w_up, "shard", scatter_dimension=0, tiled=True),
        lax.psum_scatter(grad_w_down, "shard", scatter_dimension=0, tiled=True),
    )
    summed = (
        lax.psum(parts[0].astype(jnp.bfloat16), "rep").astype(jnp.float32),
        lax.psum(parts[1].astype(jnp.bfloat16), "rep").astype(jnp.float32),
        lax.psum(parts[2].astype(jnp.bfloat16), "rep").astype(jnp.float32),
        lax.psum(parts[3].astype(jnp.bfloat16), "rep").astype(jnp.float32),
        lax.psum(parts[4].astype(jnp.bfloat16), "rep").astype(jnp.float32),
        lax.psum(parts[5].astype(jnp.bfloat16), "rep").astype(jnp.float32),
        lax.psum(parts[6].astype(jnp.bfloat16), "rep").astype(jnp.float32),
        lax.psum(parts[7].astype(jnp.bfloat16), "rep").astype(jnp.float32),
        lax.psum(parts[8].astype(jnp.bfloat16), "rep").astype(jnp.float32),
    )
    inverse_count = 1.0 / (batch_size * replicas * members)
    return (
        output,
        grad_input,
        summed[0] * inverse_count,
        summed[1] * inverse_count,
        summed[2] * inverse_count,
        summed[3] * inverse_count,
        summed[4] * inverse_count,
        summed[5] * inverse_count,
        summed[6] * inverse_count,
        summed[7] * inverse_count,
        summed[8] * inverse_count,
    )


def solution(mesh):
    return jax.shard_map(
        per_device,
        mesh=mesh,
        in_specs=(
            P(("rep", "shard"), None, None),
            P(("rep", "shard"), None),
            P("shard"),
            P("shard", None),
            P("shard", None),
            P("shard", None),
            P("shard", None),
            P("shard"),
            P("shard", None),
            P("shard", None),
            P("shard", None),
            P(("rep", "shard"), None, None),
        ),
        out_specs=(
            P(("rep", "shard"), None, None),
            P(("rep", "shard"), None, None),
            P("shard"),
            P("shard", None),
            P("shard", None),
            P("shard", None),
            P("shard", None),
            P("shard"),
            P("shard", None),
            P("shard", None),
            P("shard", None),
        ),
        check_vma=False,
    )
```

profile of v0, /device:TPU:0, one launch (start us, length us, event | category | flops | bytes accessed | tf_op | source)
XLA Modules:
  0.0 944.5 jit_solution(17049137769246098057)
XLA Ops:
  15.7 35.2 %all-reduce.5 = (bf16[768]{0:T(1024)(128)(2,1)S(1)}, bf16[768]{0:T(1024)(128)(2,1)S(1)}) all-reduce(bf16[768]{0:T(1024)(128)(2,1)S(1)} %dynamic-update-slice, bf16[768]{0:T(1024)(128)(2,1)S(1)} %dynamic-update-slice.1), channel_id=1, replica_groups=mesh['rep'=2,'shard'=16] {'shard'}, use_global_device_ids=true, to_apply=%add | all-reduce | flops 1536 | bytes 6144
  52.2 1.8 copy.39
  54.4 2.6 copy.47
  58.0 2.4 copy.40
  60.4 30.6 %all-gather.12.cloned.1.call-done = bf16[768,768]{1,0:T(8,128)(2,1)} async-done(((bf16[48,768]{1,0:T(8,128)(2,1)}), bf16[768,768]{1,0:T(8,128)(2,1)}) %all-gather.12.cloned.1.call-update) | async-done | bytes 1179664 | tf_op jit(solution)/shard_map/all_gather | solution.py:105
  91.1 2.4 copy.44
  93.4 37.2 %all-gather.10.cloned.1.call-done = bf16[768,768]{1,0:T(8,128)(2,1)} async-done(((bf16[48,768]{1,0:T(8,128)(2,1)}), bf16[768,768]{1,0:T(8,128)(2,1)}) %all-gather.10.cloned.1.call-update) | async-done | bytes 1179664 | tf_op jit(solution)/shard_map/all_gather | solution.py:104
  130.7 2.4 copy.42
  133.0 4.0 convolution_convert_fusion
  141.4 11.3 %fusion.13 = (f32[12,512]{1,0:T(8,128)}, f32[12,512,1024]{2,1,0:T(8,128)}) fusion(pred[512,1024]{1,0:T(8,128)(4,1)S(1)} %get-tuple-element.66, bf16[1024,12,32]{0,2,1:T(8,128)(2,1)S(1)} %get-tuple-element.58, bf16[1024,12,32]{0,2,1:T(8,128)(2,1)S(1)} %get-tuple-element.57, bf16[1,1024,12,32]{1,3,2,0:T(8,128)(2,1)S(1)} %get-tuple-element.63, ...), kind=kOutput, calls=%fused_computation.23 | convolution fusion | flops 828893184 | bytes 28860416 | tf_op jit(solution)/shard_map/bqhd,bkhd->bhqk/dot_general | solution.py:76
  152.7 14.6 %fusion.12 = (f32[12,512]{1,0:T(8,128)}, f32[12,512,1024]{2,1,0:T(8,128)}) fusion(pred[512,1024]{1,0:T(8,128)(4,1)S(1)} %get-tuple-element.65, bf16[1024,12,32]{0,2,1:T(8,128)(2,1)} %copy-done.10, bf16[1024,12,32]{0,2,1:T(8,128)(2,1)} %copy-done.8, bf16[1,1024,12,32]{1,3,2,0:T(8,128)(2,1)} %copy-done.3, bf16[1,1024,12,32]{1,3,2,0:T(8,128)(2,1)} %copy-done.1), kind=kOutput, calls=%fused_computation.22 | convolution fusion | flops 828893184 | bytes 28860416 | tf_op jit(solution)/shard_map/bqhd,bkhd->bhqk/dot_general | solution.py:76
  167.3 12.8 %fusion.1 = f32[12,512]{1,0:T(8,128)S(1)} fusion(f32[12,512]{1,0:T(8,128)} %get-tuple-element.73, f32[12,512,1024]{2,1,0:T(8,128)} %get-tuple-element.74, pred[512,1024]{1,0:T(8,128)(4,1)S(1)} %get-tuple-element.66), kind=kLoop, calls=%fused_computation.13 | loop fusion | flops 25159680 | bytes 25739264 | tf_op jit(solution)/shard_map/reduce_sum | solution.py:135
  180.3 8.7 fusion.49
  188.9 13.4 %fusion = f32[12,512]{1,0:T(8,128)S(1)} fusion(f32[12,512]{1,0:T(8,128)} %get-tuple-element.75, f32[12,512,1024]{2,1,0:T(8,128)} %get-tuple-element.76, pred[512,1024]{1,0:T(8,128)(4,1)S(1)} %get-tuple-element.65), kind=kLoop, calls=%fused_computation.12 | loop fusion | flops 25159680 | bytes 25739264 | tf_op jit(solution)/shard_map/reduce_sum | solution.py:135
  202.4 2.5 copy-done
  204.9 9.2 fusion.48
  215.5 3.4 multiply_reduce_fusion.4
  219.0 1.6 copy-done.5
  222.1 9.1 fusion.97
  231.1 31.5 %all-gather.16.cloned.1.call-done = bf16[768,2048]{1,0:T(8,128)(2,1)} async-done(((bf16[48,2048]{1,0:T(8,128)(2,1)}), bf16[768,2048]{1,0:T(8,128)(2,1)}) %all-gather.16.cloned.1.call-update) | async-done | bytes 3145744 | tf_op jit(solution)/shard_map/all_gather | solution.py:109
  262.6 9.1 fusion.96
  271.7 37.2 %all-gather.20.cloned.1.call-done = bf16[2048,768]{1,0:T(8,128)(2,1)} async-done(((bf16[128,768]{1,0:T(8,128)(2,1)}), bf16[2048,768]{1,0:T(8,128)(2,1)}) %all-gather.20.cloned.1.call-update) | async-done | bytes 3145744 | tf_op jit(solution)/shard_map/all_gather | solution.py:111
  309.0 14.4 %multiply_convert_fusion.2 = (bf16[1024,2048]{1,0:T(8,128)(2,1)S(1)}, bf16[1024,2048]{1,0:T(8,128)(2,1)}, bf16[1024,2048]{1,0:T(8,128)(2,1)}) fusion(f32[1024,2048]{1,0:T(8,128)} %fusion.96, f32[1024,2048]{1,0:T(8,128)} %fusion.97, bf16[2048,768]{1,0:T(8,128)(2,1)} %all-gather.20.cloned.1.call-done, bf16[1,1024,768]{2,1,0:T(8,128)(2,1)} %param.23), kind=kOutput, calls=%fused_computation.24 | convolution fusion | flops 3254779904 | bytes 34078720 | tf_op jit(solution)/shard_map/dot_general | solution.py:64
  323.4 7.4 fusion.98
  330.8 4.6 multiply_reduce_fusion.2
  336.2 1.6 copy-done.7
  337.8 2.9 fusion.55
  340.8 3.6 convolution_convert_fusion.1
  344.5 12.4 %fusion.4 = f32[12,64,1024]{2,1,0:T(8,128)S(1)} fusion(f32[12,512]{1,0:T(8,128)S(1)} %log_add_fusion, f32[12,512,1024]{2,1,0:T(8,128)} %get-tuple-element.74, pred[512,1024]{1,0:T(8,128)(4,1)S(1)} %get-tuple-element.66, bf16[1,1024,12,64]{1,3,2,0:T(8,128)(2,1)S(1)} %bitcast.182), kind=kOutput, calls=%fused_computation.16 | convolution fusion | flops 830472192 | bytes 29655040 | tf_op jit(solution)/shard_map/bhqk,bqhd->bkhd/dot_general | solution.py:195
  357.0 11.8 %add_convert_fusion = bf16[12,64,1024]{2,1,0:T(8,128)(2,1)S(1)} fusion(f32[12,64,1024]{2,1,0:T(8,128)S(1)} %fusion.4, f32[12,512]{1,0:T(8,128)S(1)} %log_add_fusion.1, f32[12,512,1024]{2,1,0:T(8,128)} %get-tuple-element.76, pred[512,1024]{1,0:T(8,128)(4,1)S(1)} %get-tuple-element.65, bf16[1,1024,12,64]{1,3,2,0:T(8,128)(2,1)S(1)} %bitcast.183), kind=kOutput, calls=%fused_computation.50 | convolution fusion | flops 832045056 | bytes 31227904 | tf_op jit(solution)/shard_map/bhqk,bqhd->bkhd/dot_general | solution.py:195
  370.0 2.9 fusion.41
  372.9 18.2 %multiply_reduce_fusion = (f32[12,512]{1,0:T(8,128)S(1)}, f32[12,512,1024]{2,1,0:T(8,128)}) fusion(f32[12,512]{1,0:T(8,128)S(1)} %log_add_fusion, f32[12,512,1024]{2,1,0:T(8,128)} %get-tuple-element.74, pred[512,1024]{1,0:T(8,128)(4,1)S(1)} %get-tuple-element.66, bf16[1024,12,64]{0,2,1:T(8,128)(2,1)} %convolution_convert_fusion, ...), kind=kOutput, calls=%fused_computation.1 | convolution fusion | flops 836757504 | bytes 53264384 | tf_op jit(solution)/shard_map/bqhd,bkhd->bhqk/dot_general | solution.py:198
  391.1 18.2 %multiply_reduce_fusion.1 = (f32[12,512]{1,0:T(8,128)S(1)}, f32[12,512,1024]{2,1,0:T(8,128)}) fusion(f32[12,512]{1,0:T(8,128)S(1)} %log_add_fusion.1, f32[12,512,1024]{2,1,0:T(8,128)} %get-tuple-element.76, pred[512,1024]{1,0:T(8,128)(4,1)S(1)} %get-tuple-element.65, bf16[1024,12,64]{0,2,1:T(8,128)(2,1)} %convolution_convert_fusion, ...), kind=kOutput, calls=%fused_computation.4 | convolution fusion | flops 836757504 | bytes 53264384 | tf_op jit(solution)/shard_map/bqhd,bkhd->bhqk/dot_general | solution.py:198
  409.4 43.6 %multiply_convert_fusion = (bf16[12,512,1024]{2,1,0:T(8,128)(2,1)}, bf16[12,512,1024]{2,1,0:T(8,128)(2,1)}) fusion(f32[12,512,1024]{2,1,0:T(8,128)} %get-tuple-element.83, f32[12,512]{1,0:T(8,128)S(1)} %get-tuple-element.82, f32[12,512]{1,0:T(8,128)S(1)} %log_add_fusion, f32[12,512,1024]{2,1,0:T(8,128)} %get-tuple-element.74, ...), kind=kLoop, calls=%fused_computation | loop fusion | flops 75497472 | bytes 126976000 | tf_op jit(solution)/shard_map/convert_element_type | solution.py:203
  453.1 7.1 fusion.85
  460.1 9.7 %multiply_bitcast_fusion.2 = f32[1,512,12,64]{1,3,2,0:T(8,128)} fusion(bf16[12,512,1024]{2,1,0:T(8,128)(2,1)} %get-tuple-element.86, bf16[1024,12,32]{0,2,1:T(8,128)(2,1)S(1)} %copy-done.11, bf16[1024,12,32]{0,2,1:T(8,128)(2,1)S(1)} %copy-done.9), kind=kOutput, calls=%fused_computation.89 | convolution fusion | flops 808845312 | bytes 15728640 | tf_op jit(solution)/shard_map/bhqk,bkhd->bqhd/dot_general | solution.py:205
  469.8 9.7 %multiply_bitcast_fusion.1 = f32[1,512,12,64]{1,3,2,0:T(8,128)} fusion(bf16[12,512,1024]{2,1,0:T(8,128)(2,1)} %get-tuple-element.85, bf16[1024,12,32]{0,2,1:T(8,128)(2,1)S(1)} %copy-done.11, bf16[1024,12,32]{0,2,1:T(8,128)(2,1)S(1)} %copy-done.9), kind=kOutput, calls=%fused_computation.88 | convolution fusion | flops 808845312 | bytes 15728640 | tf_op jit(solution)/shard_map/bhqk,bkhd->bqhd/dot_general | solution.py:205
  479.6 7.1 multiply_bitcast_fusion
  489.3 2.9 fusion.43
  493.6 2.9 fusion.39
  496.6 8.9 fusion.100
  505.6 8.9 fusion.99
  514.6 8.8 fusion.32
  524.3 8.7 fusion.45
  533.0 2.6 copy.53
  535.6 3.3 fusion.101
  540.7 3.6 fusion.25
  544.3 31.8 %all-reduce.4 = (bf16[768]{0:T(1024)(128)(2,1)S(1)}, bf16[768]{0:T(1024)(128)(2,1)S(1)}) all-reduce(f32[768]{0:T(1024)S(1)} %get-tuple-element.35, f32[768]{0:T(1024)S(1)} %copy-done.42), channel_id=2, replica_groups=mesh['rep'=2,'shard'=16] {'shard'}, use_global_device_ids=true, to_apply=%region_11.12.clone | all-reduce | flops 1536 | bytes 9216
  576.3 1.6 convert_element_type.235
  581.0 39.4 %reduce-scatter.10.cloned.1.call-done = f32[48,768]{1,0:T(8,128)} async-done(((f32[768,768]{1,0:T(8,128)}), f32[48,768]{1,0:T(8,128)}) %reduce-scatter.10.cloned.1.call-update) | async-done | bytes 147472 | tf_op jit(solution)/shard_map/reduce_scatter | solution.py:244
  621.9 86.6 %reduce-scatter.18.cloned.1.call-done = f32[48,2048]{1,0:T(8,128)} async-done(((f32[768,2048]{1,0:T(8,128)}), f32[48,2048]{1,0:T(8,128)}) %reduce-scatter.18.cloned.1.call-update) | async-done | bytes 393232 | tf_op jit(solution)/shard_map/reduce_scatter | solution.py:249
  708.5 1.7 convert_element_type.241
  710.2 87.3 %reduce-scatter.16.cloned.1.call-done = f32[48,2048]{1,0:T(8,128)} async-done(((f32[768,2048]{1,0:T(8,128)}), f32[48,2048]{1,0:T(8,128)}) %reduce-scatter.16.cloned.1.call-update) | async-done | bytes 393232 | tf_op jit(solution)/shard_map/reduce_scatter | solution.py:248
  797.5 1.7 convert_element_type.239
  799.2 86.5 %reduce-scatter.20.cloned.1.call-done = f32[128,768]{1,0:T(8,128)} async-done(((f32[2048,768]{1,0:T(8,128)}), f32[128,768]{1,0:T(8,128)}) %reduce-scatter.20.cloned.1.call-update) | async-done | bytes 393232 | tf_op jit(solution)/shard_map/reduce_scatter | solution.py:250
  885.7 1.7 convert_element_type.243
  887.4 5.3 fusion.24
  892.7 3.7 copy.54
  896.4 5.0 all-reduce.6
  902.4 24.1 %all-reduce.10.cloned.1.call-done = (bf16[48,768]{1,0:T(8,128)(2,1)}, bf16[48,768]{1,0:T(8,128)(2,1)}, bf16[48,768]{1,0:T(8,128)(2,1)}, bf16[48,768]{1,0:T(8,128...) async-done(((bf16[48,768]{1,0:T(8,128)(2,1)}, bf16[48,768]{1,0:T(8,128)(2,1)}, bf16[48,768]{1,0:T(8,128)(2,1)}, ...) | async-done | bytes 884752 | tf_op jit(solution)/shard_map/psum | solution.py:254
  926.5 1.6 convert_multiply_fusion.7
  932.7 1.7 convert_multiply_fusion.3
  934.4 1.7 convert_multiply_fusion.2
  936.1 1.7 convert_multiply_fusion.1
  (179 shorter events, 36.3 us)
Async XLA Ops:
  7.2 50.8 %all-gather.8.cloned.1.call-start = ((), (), s32[]{:S(2)}) async-start(), calls=%async_computation.7 | async-start | bytes 1253376 | tf_op jit(solution)/shard_map/all_gather | solution.py:106
  7.9 83.1 %all-gather.12.cloned.1.call-start = ((), (), s32[]{:S(2)}) async-start(), calls=%async_computation.9 | async-start | bytes 1253376 | tf_op jit(solution)/shard_map/all_gather | solution.py:105
  8.7 122.0 %all-gather.10.cloned.1.call-start = ((), (), s32[]{:S(2)}) async-start(), calls=%async_computation.8 | async-start | bytes 1253376 | tf_op jit(solution)/shard_map/all_gather | solution.py:104
  9.4 206.1 %all-gather.14.cloned.1.call-start = ((), (), s32[]{:S(2)}) async-start(), calls=%async_computation.10 | async-start | bytes 1253376 | tf_op jit(solution)/shard_map/all_gather | solution.py:107
  10.0 212.1 %all-gather.18.cloned.1.call-start = ((), (), s32[]{:S(2)}) async-start(), calls=%async_computation.12 | async-start | bytes 3342336 | tf_op jit(solution)/shard_map/all_gather | solution.py:110
  10.6 252.1 %all-gather.16.cloned.1.call-start = ((), (), s32[]{:S(2)}) async-start(), calls=%async_computation.11 | async-start | bytes 3342336 | tf_op jit(solution)/shard_map/all_gather | solution.py:109
  11.1 297.8 %all-gather.20.cloned.1.call-start = ((), (), s32[]{:S(2)}) async-start(), calls=%async_computation.13 | async-start | bytes 3342336 | tf_op jit(solution)/shard_map/all_gather | solution.py:111
  11.9 564.4 %reduce-scatter.14.cloned.1.call-start = ((), (), s32[]{:S(2)}) async-start(), calls=%async_computation.17 | async-start | bytes 2506752 | tf_op jit(solution)/shard_map/reduce_scatter | solution.py:246
  50.9 87.7 %copy-start.37 = (f32[768]{0:T(1024)}, f32[768]{0:T(1024)S(1)}, u32[]{:S(2)}) copy-start(f32[768]{0:T(1024)S(1)} %convert_element_type.200) | copy-start | bytes 9220
  52.2 88.0 %copy-start.24 = (f32[1024,32]{0,1:T(8,128)}, f32[1024,32]{0,1:T(8,128)S(1)}, u32[]{:S(2)}) copy-start(f32[1024,32]{0,1:T(8,128)S(1)} %get-tuple-element.71) | copy-start | bytes 393220
  52.2 88.0 %copy-start.26 = (f32[1024,32]{0,1:T(8,128)}, f32[1024,32]{0,1:T(8,128)S(1)}, u32[]{:S(2)}) copy-start(f32[1024,32]{0,1:T(8,128)S(1)} %get-tuple-element.72) | copy-start | bytes 393220
  54.0 3.0 copy-start.41
  54.4 84.3 %copy-start.39 = (f32[1024]{0:T(1024)}, f32[1024]{0:T(1024)S(1)}, u32[]{:S(2)}) copy-start(f32[1024]{0:T(1024)S(1)} %add_rsqrt_fusion.1) | copy-start | bytes 12292
  133.0 4.0 copy-start.29
  137.1 1.6 copy-start.30
  141.4 11.3 %copy-start.1 = (bf16[1,1024,12,32]{1,3,2,0:T(8,128)(2,1)}, bf16[1,1024,12,32]{1,3,2,0:T(8,128)(2,1)S(1)}, u32[]{:S(2)}) copy-start(bf16[1,1024,12,32]{1,3,2,0:T(8,128)(2,1)S(1)} %get-tuple-element.63) | copy-start | bytes 2359300
  141.4 11.3 %copy-start.3 = (bf16[1,1024,12,32]{1,3,2,0:T(8,128)(2,1)}, bf16[1,1024,12,32]{1,3,2,0:T(8,128)(2,1)S(1)}, u32[]{:S(2)}) copy-start(bf16[1,1024,12,32]{1,3,2,0:T(8,128)(2,1)S(1)} %get-tuple-element.64) | copy-start | bytes 2359300
  141.4 11.3 %copy-start.8 = (bf16[1024,12,32]{0,2,1:T(8,128)(2,1)}, bf16[1024,12,32]{0,2,1:T(8,128)(2,1)S(1)}, u32[]{:S(2)}) copy-start(bf16[1024,12,32]{0,2,1:T(8,128)(2,1)S(1)} %get-tuple-element.57) | copy-start | bytes 2359300
  141.4 11.3 %copy-start.10 = (bf16[1024,12,32]{0,2,1:T(8,128)(2,1)}, bf16[1024,12,32]{0,2,1:T(8,128)(2,1)S(1)}, u32[]{:S(2)}) copy-start(bf16[1024,12,32]{0,2,1:T(8,128)(2,1)S(1)} %get-tuple-element.58) | copy-start | bytes 2359300
  152.7 27.5 %slice-start = ((s8[25165824]{0:T(1024)(128)(4,1)}), s8[4194304]{0:T(1024)(128)(4,1)S(1)}, s32[]{:S(2)}) async-start(s8[25165824]{0:T(1024)(128)(4,1)} %bitcast.171), calls=%async_computation.22 | async-start | bytes 8388608
  152.7 27.5 %slice-start.1 = ((s8[25165824]{0:T(1024)(128)(4,1)}), s8[4194304]{0:T(1024)(128)(4,1)S(1)}, s32[]{:S(2)}) async-start(s8[25165824]{0:T(1024)(128)(4,1)} %bitcast.171), calls=%async_computation.23 | async-start | bytes 8388608
  152.7 27.5 %slice-start.2 = ((s8[25165824]{0:T(1024)(128)(4,1)}), s8[4194304]{0:T(1024)(128)(4,1)S(1)}, s32[]{:S(2)}) async-start(s8[25165824]{0:T(1024)(128)(4,1)} %bitcast.171), calls=%async_computation.24 | async-start | bytes 8388608
  152.7 27.5 %slice-start.3 = ((s8[25165824]{0:T(1024)(128)(4,1)}), s8[4194304]{0:T(1024)(128)(4,1)S(1)}, s32[]{:S(2)}) async-start(s8[25165824]{0:T(1024)(128)(4,1)} %bitcast.171), calls=%async_computation.25 | async-start | bytes 8388608
  167.3 12.9 %slice-start.4 = ((s8[25165824]{0:T(1024)(128)(4,1)}), s8[4194304]{0:T(1024)(128)(4,1)S(1)}, s32[]{:S(2)}) async-start(s8[25165824]{0:T(1024)(128)(4,1)} %bitcast.171), calls=%async_computation.26 | async-start | bytes 8388608
  167.3 12.9 %slice-start.5 = ((s8[25165824]{0:T(1024)(128)(4,1)}), s8[4194304]{0:T(1024)(128)(4,1)S(1)}, s32[]{:S(2)}) async-start(s8[25165824]{0:T(1024)(128)(4,1)} %bitcast.171), calls=%async_computation.27 | async-start | bytes 8388608
  167.3 12.9 %copy-start.12 = (bf16[1024,12,64]{0,2,1:T(8,128)(2,1)S(1)}, bf16[1024,12,64]{0,2,1:T(8,128)(2,1)}, u32[]{:S(2)}) copy-start(bf16[1024,12,64]{0,2,1:T(8,128)(2,1)} %convolution_convert_fusion) | copy-start | bytes 4718596
  167.3 12.9 %copy-start.32 = (f32[12,512]{1,0:T(8,128)S(1)}, f32[12,512]{1,0:T(8,128)}, u32[]{:S(2)}) copy-start(f32[12,512]{1,0:T(8,128)} %get-tuple-element.73) | copy-start | bytes 73732
  180.3 8.7 copy-start.35
  188.9 15.9 %copy-start = (f32[12,512,1024]{2,1,0:T(8,128)S(1)}, f32[12,512,1024]{2,1,0:T(8,128)}, u32[]{:S(2)}) copy-start(f32[12,512,1024]{2,1,0:T(8,128)} %get-tuple-element.76) | copy-start | bytes 75497472
  188.9 15.9 %copy-start.34 = (f32[12,512]{1,0:T(8,128)S(1)}, f32[12,512]{1,0:T(8,128)}, u32[]{:S(2)}) copy-start(f32[12,512]{1,0:T(8,128)} %get-tuple-element.75) | copy-start | bytes 73732
  204.9 9.2 copy-start.31
  215.5 3.4 copy-start.33
  215.5 3.5 copy-start.36
  218.9 1.7 copy-start.5
  308.9 14.4 %copy-start.44 = (bf16[768,2048]{1,0:T(8,128)(2,1)S(1)}, bf16[768,2048]{1,0:T(8,128)(2,1)}, u32[]{:S(2)}) copy-start(bf16[768,2048]{1,0:T(8,128)(2,1)} %all-gather.16.cloned.1.call-done) | copy-start | bytes 9437188
  323.4 7.4 copy-start.45
  323.4 7.4 copy-start.6
  323.4 7.4 copy-start.43
  330.8 4.6 copy-start.13
  335.4 2.4 copy-start.20
  336.2 1.6 copy-start.7
  340.8 237.1 %reduce-scatter.12.cloned.1.call-start = ((), (), s32[]{:S(2)}) async-start(), calls=%async_computation.16 | async-start | bytes 2506752 | tf_op jit(solution)/shard_map/reduce_scatter | solution.py:245
  344.5 12.4 %copy-start.23 = (bf16[1024,768]{0,1:T(8,128)(2,1)}, bf16[1024,768]{0,1:T(8,128)(2,1)S(1)}, u32[]{:S(2)}) copy-start(bf16[1024,768]{0,1:T(8,128)(2,1)S(1)} %convolution_convert_fusion.1) | copy-start | bytes 4718596
  356.9 13.1 %copy-start.38 = (f32[768]{0:T(1024)S(1)}, f32[768]{0:T(1024)}, u32[]{:S(2)}) copy-start(f32[768]{0:T(1024)} %copy-done.37) | copy-start | bytes 9220
  356.9 13.1 %copy-start.40 = (f32[1024]{0:T(1024)S(1)}, f32[1024]{0:T(1024)}, u32[]{:S(2)}) copy-start(f32[1024]{0:T(1024)} %copy-done.39) | copy-start | bytes 12292
  409.3 170.1 %reduce-scatter.8.cloned.1.call-start = ((), (), s32[]{:S(2)}) async-start(), calls=%async_computation.14 | async-start | bytes 2506752 | tf_op jit(solution)/shard_map/reduce_scatter | solution.py:243
  409.4 43.6 %copy-start.2 = (bf16[1,1024,12,32]{1,3,2,0:T(8,128)(2,1)S(1)}, bf16[1,1024,12,32]{1,3,2,0:T(8,128)(2,1)}, u32[]{:S(2)}) copy-start(bf16[1,1024,12,32]{1,3,2,0:T(8,128)(2,1)} %copy-done.1) | copy-start | bytes 2359300
  409.4 43.6 %copy-start.4 = (bf16[1,1024,12,32]{1,3,2,0:T(8,128)(2,1)S(1)}, bf16[1,1024,12,32]{1,3,2,0:T(8,128)(2,1)}, u32[]{:S(2)}) copy-start(bf16[1,1024,12,32]{1,3,2,0:T(8,128)(2,1)} %copy-done.3) | copy-start | bytes 2359300
  453.0 7.1 copy-start.9
  453.0 7.1 copy-start.11
  479.5 7.2 copy-start.14
  479.5 7.2 copy-start.15
  479.5 7.2 copy-start.25
  479.6 7.2 copy-start.27
  492.3 128.1 %reduce-scatter.10.cloned.1.call-start = ((), (), s32[]{:S(2)}) async-start(), calls=%async_computation.15 | async-start | bytes 2506752 | tf_op jit(solution)/shard_map/reduce_scatter | solution.py:244
  496.6 211.9 %reduce-scatter.18.cloned.1.call-start = ((), (), s32[]{:S(2)}) async-start(), calls=%async_computation.19 | async-start | bytes 6684672 | tf_op jit(solution)/shard_map/reduce_scatter | solution.py:249
  505.6 291.9 %reduce-scatter.16.cloned.1.call-start = ((), (), s32[]{:S(2)}) async-start(), calls=%async_computation.18 | async-start | bytes 6684672 | tf_op jit(solution)/shard_map/reduce_scatter | solution.py:248
  514.6 371.1 %reduce-scatter.20.cloned.1.call-start = ((), (), s32[]{:S(2)}) async-start(), calls=%async_computation.20 | async-start | bytes 6684672 | tf_op jit(solution)/shard_map/reduce_scatter | solution.py:250
  523.4 403.0 %all-reduce.10.cloned.1.call-start = ((), (), s32[]{:S(2)}) async-start(), calls=%async_computation.21 | async-start | bytes 1769472 | tf_op jit(solution)/shard_map/psum | solution.py:254
  535.6 3.3 copy-start.19
  535.6 3.3 copy-start.28
  538.9 1.4 copy-start.16
  538.9 1.8 copy-start.22
  540.7 3.6 copy-start.42
  (3 other events, 3.6 us)
Sparse Core Ops, SparseCore 0:
  10.3 41.1 all-gather.7
  53.7 37.2 all-gather.11
  93.3 37.2 all-gather.9
  132.8 37.3 all-gather.13
  172.3 44.1 all-gather.17
  218.6 43.9 all-gather.15
  264.9 43.9 all-gather.19
  340.9 61.7 reduce-scatter.13
  409.4 61.8 reduce-scatter.11
  492.4 61.8 reduce-scatter.7
  558.5 61.8 reduce-scatter.9
  624.2 84.2 reduce-scatter.17
  713.0 84.4 reduce-scatter.15
  801.3 84.3 reduce-scatter.19
  889.6 36.7 all-reduce.9
where the time goes:
time: 954 us; the launch traced here: 945 us
  waiting for transfers between devices  465 us (49%)
  matrix products  252 us (26%)
  other arithmetic  107 us (11%)
  blocking collectives  72 us (8%)
  local copies, waits for them, and re-layouts  31.4 us (3%)
  between operations  16.3 us (2%)
    reduce_scatter x1, waiting for transfers between devices, per_device(): lax.psum_scatter(grad_w_gate, 'shard', scatter_dimension=0, tiled=True)  87.3 us
    reduce_scatter x1, waiting for transfers between devices, per_device(): lax.psum_scatter(grad_w_up, 'shard', scatter_dimension=0, tiled=True)  86.6 us
    reduce_scatter x1, waiting for transfers between devices, per_device(): lax.psum_scatter(grad_w_down, 'shard', scatter_dimension=0, tiled=True)  86.5 us
    unnamed x2, blocking collectives  67.1 us
    convert_element_type x1, other arithmetic, per_device(): grad_scores = (probs_full * (grad_probs - jnp.sum(probs_full * grad_probs...  43.6 us
    reduce_scatter x1, waiting for transfers between devices, per_device(): lax.psum_scatter(grad_w_key, 'shard', scatter_dimension=0, tiled=True)  39.4 us
    dot_general x7, matrix products, right_transposed(): lax.dot_general(left, right, (((1,), (1,)), ((), ())), preferred_element_...  38.3 us
    dot_general x7, matrix products, rows_product(): lax.dot_general(left, right, (((0,), (0,)), ((), ())), preferred_element_...  38.2 us
  transfers between devices with their start and end apart: 15, of which 9 were waited for; matrix products, arithmetic and copies ran while one was open for 36% of the time, Pallas kernels for 0%

commit v1 on v0

--- a/solution.py
+++ b/solution.py
@@ -9,6 +9,28 @@
 epsilon = 1e-06
 rope_base = 10000.0
 masked_score = -1e30
+
+
+def laid_out(blocks, dim):
+    lengths = list(blocks.shape[1:])
+    lengths[dim] *= blocks.shape[0]
+    return jnp.moveaxis(blocks, 0, dim).reshape(lengths)
+
+
+def ring_gather(shard, axis, dim):
+    peers = lax.axis_size(axis)
+    pairs = [(i, (i + 1) % peers) for i in range(peers)]
+    back = [(b, a) for a, b in pairs]
+    lower, upper = ([], [])
+    for step in range(peers - 1):
+        if step % 2 == 0:
+            lower.append(lax.ppermute(lower[-1] if lower else shard, axis, pairs))
+        else:
+            upper.append(lax.ppermute(upper[-1] if upper else shard, axis, back))
+    parts = jnp.stack([*lower[::-1], shard, *upper])
+    shift = lax.axis_index(axis) - len(lower)
+    parts = parts[(jnp.arange(peers) - shift) % peers]
+    return laid_out(parts, dim)
 
 
 def rope_tables(length, head_size):
@@ -102,7 +124,7 @@
     gain_one, query_mat, key_mat, value_mat, out_mat, gain_two, gate_mat, up_mat, down_mat = (
         lax.all_gather(attn_gain, "shard", axis=0, tiled=True),
         lax.all_gather(w_query, "shard", axis=0, tiled=True),
-        lax.all_gather(w_key, "shard", axis=0, tiled=True),
+        ring_gather(w_key, "shard", 0),
         lax.all_gather(w_value, "shard", axis=0, tiled=True),
         lax.all_gather(w_out, "shard", axis=0, tiled=True),
         lax.all_gather(ffn_gain, "shard", axis=0, tiled=True),

time: 954 us -> 925 us (0.970)
  waiting for transfers between devices: 465 us -> 395 us
  starting transfers between devices: 0.81 us -> 30 us
  local copies, waits for them, and re-layouts: 31.4 us -> 47.5 us
    all_gather x1, waiting for transfers between devices: 37.2 us -> 0.01 us  [per_device(): lax.all_gather(w_query, 'shard', axis=0, tiled=True)]
    all_gather x1, waiting for transfers between devices: 30.6 us -> 0.01 us  [per_device(): lax.all_gather(w_key, 'shard', axis=0, tiled=True)]
    ppermute x0 -> x15, starting transfers between devices: none -> 29.3 us  [the longest x7 28.2 us: ring_gather(): upper.append(lax.ppermute(upper[-1] if upper else shard, axis, back))]
    all_gather x1, waiting for transfers between devices: 31.5 us -> 4.06 us  [per_device(): lax.all_gather(w_gate, 'shard', axis=0, tiled=True)]
    ppermute x0 -> x15, waiting for transfers between devices: none -> 14.7 us  [the longest x8 8.77 us: ring_gather(): lower.append(lax.ppermute(lower[-1] if lower else shard, axis, pairs))]
    unnamed x115 -> x122, local copies, waits for them, and re-layouts: 23.6 us -> 36.1 us
    reduce_scatter x1, waiting for transfers between devices: 39.4 us -> 51.2 us  [per_device(): lax.psum_scatter(grad_w_key, 'shard', scatter_dimension=0, tiled=True)]
  transfers between devices with their start and end apart: 15 -> 30, of which waited for: 9 -> 13; matrix products, arithmetic and copies ran while one was open for 36% -> 41% of each run, Pallas kernels for 0% -> 0%
where the time goes in v1:
time: 925 us; the launch traced here: 919 us
  waiting for transfers between devices  395 us (43%)
  matrix products  252 us (27%)
  other arithmetic  108 us (12%)
  blocking collectives  71.1 us (8%)
  local copies, waits for them, and re-layouts  47.5 us (5%)
  starting transfers between devices  30 us (3%)
  between operations  16.1 us (2%)
    reduce_scatter x1, waiting for transfers between devices, per_device(): lax.psum_scatter(grad_w_gate, 'shard', scatter_dimension=0, tiled=True)  87.4 us
    reduce_scatter x1, waiting for transfers between devices, per_device(): lax.psum_scatter(grad_w_up, 'shard', scatter_dimension=0, tiled=True)  86.5 us
    reduce_scatter x1, waiting for transfers between devices, per_device(): lax.psum_scatter(grad_w_down, 'shard', scatter_dimension=0, tiled=True)  86.5 us
    unnamed x2, blocking collectives  66.1 us
    reduce_scatter x1, waiting for transfers between devices, per_device(): lax.psum_scatter(grad_w_key, 'shard', scatter_dimension=0, tiled=True)  51.2 us
    convert_element_type x1, other arithmetic, per_device(): grad_scores = (probs_full * (grad_probs - jnp.sum(probs_full * grad_probs...  42.8 us
    dot_general x7, matrix products, right_transposed(): lax.dot_general(left, right, (((1,), (1,)), ((), ())), preferred_element_...  38.9 us
    dot_general x7, matrix products, rows_product(): lax.dot_general(left, right, (((0,), (0,)), ((), ())), preferred_element_...  37.4 us
  transfers between devices with their start and end apart: 30, of which 13 were waited for; matrix products, arithmetic and copies ran while one was open for 41% of the time, Pallas kernels for 0%

profile of v1, /device:TPU:0, one launch (start us, length us, event | category | flops | bytes accessed | tf_op | source)
XLA Modules:
  0.0 919.3 jit_solution(17358592879348087035)
XLA Ops:
  11.7 5.1 collective-permute-start.8
  20.8 4.9 collective-permute-done.1
  25.7 4.5 collective-permute-start.9
  30.2 2.4 collective-permute-done.2
  35.5 4.5 collective-permute-start.10
  42.4 4.6 collective-permute-start.11
  48.7 34.0 %all-reduce.5 = (bf16[768]{0:T(1024)(128)(2,1)S(1)}, bf16[768]{0:T(1024)(128)(2,1)S(1)}) all-reduce(bf16[768]{0:T(1024)(128)(2,1)S(1)} %dynamic-update-slice, bf16[768]{0:T(1024)(128)(2,1)S(1)} %dynamic-update-slice.1), channel_id=1, replica_groups=mesh['rep'=2,'shard'=16] {'shard'}, use_global_device_ids=true, to_apply=%add | all-reduce | flops 1536 | bytes 6144
  82.8 2.6 copy.47
  85.9 2.0 collective-permute-done.12
  88.0 4.6 collective-permute-start.13
  94.5 5.0 collective-permute-start.14
  110.6 2.9 gather_fusion
  113.5 2.4 copy.44
  115.9 4.4 convolution_bitcast_fusion
  120.3 2.4 copy.40
  122.7 2.4 copy.42
  125.1 4.0 convolution_convert_fusion
  132.2 10.8 %fusion.13 = (f32[12,512]{1,0:T(8,128)S(1)}, f32[12,512,1024]{2,1,0:T(8,128)}) fusion(pred[512,1024]{1,0:T(8,128)(4,1)S(1)} %get-tuple-element.66, bf16[1024,12,32]{0,2,1:T(8,128)(2,1)S(1)} %get-tuple-element.58, bf16[1024,12,32]{0,2,1:T(8,128)(2,1)S(1)} %get-tuple-element.57, bf16[1,1024,12,32]{1,3,2,0:T(8,128)(2,1)S(1)} %get-tuple-element.63, ...), kind=kOutput, calls=%fused_computation.24 | convolution fusion | flops 828893184 | bytes 28860416 | tf_op jit(solution)/shard_map/bqhd,bkhd->bhqk/dot_general | solution.py:98
  142.9 12.4 %fusion.1 = f32[12,512]{1,0:T(8,128)S(1)} fusion(f32[12,512]{1,0:T(8,128)S(1)} %get-tuple-element.73, f32[12,512,1024]{2,1,0:T(8,128)} %get-tuple-element.74, pred[512,1024]{1,0:T(8,128)(4,1)S(1)} %get-tuple-element.66), kind=kLoop, calls=%fused_computation.14 | loop fusion | flops 25159680 | bytes 25739264 | tf_op jit(solution)/shard_map/reduce_sum | solution.py:157
  155.9 2.5 copy-done
  158.4 9.6 %fusion.49 = bf16[1,512,12,64]{1,3,2,0:T(8,128)(2,1)} fusion(bf16[1024,12,64]{0,2,1:T(8,128)(2,1)} %convolution_convert_fusion, f32[12,512]{1,0:T(8,128)S(1)} %fusion.1, f32[12,512]{1,0:T(8,128)S(1)} %get-tuple-element.73, f32[12,512,1024]{2,1,0:T(8,128)S(1)} %copy-done, pred[512,1024]{1,0:T(8,128)(4,1)S(1)} %get-tuple-element.66), kind=kOutput, calls=%fused_computation.99 | convolution fusion | flops 837156864 | bytes 28098560 | tf_op jit(solution)/shard_map/bhqk,bkhd->bqhd/dot_general | solution.py:161
  168.0 12.1 %fusion.12 = (f32[12,512]{1,0:T(8,128)S(1)}, f32[12,512,1024]{2,1,0:T(8,128)}) fusion(pred[512,1024]{1,0:T(8,128)(4,1)S(1)} %get-tuple-element.65, bf16[1024,12,32]{0,2,1:T(8,128)(2,1)} %copy-done.11, bf16[1024,12,32]{0,2,1:T(8,128)(2,1)S(1)} %get-tuple-element.57, bf16[1,1024,12,32]{1,3,2,0:T(8,128)(2,1)S(1)} %get-tuple-element.64, ...), kind=kOutput, calls=%fused_computation.23 | convolution fusion | flops 828893184 | bytes 28860416 | tf_op jit(solution)/shard_map/bqhd,bkhd->bhqk/dot_general | solution.py:98
  180.2 12.4 %fusion = f32[12,512]{1,0:T(8,128)S(1)} fusion(f32[12,512]{1,0:T(8,128)S(1)} %get-tuple-element.75, f32[12,512,1024]{2,1,0:T(8,128)} %get-tuple-element.76, pred[512,1024]{1,0:T(8,128)(4,1)S(1)} %get-tuple-element.65), kind=kLoop, calls=%fused_computation.13 | loop fusion | flops 25159680 | bytes 25739264 | tf_op jit(solution)/shard_map/reduce_sum | solution.py:157
  192.6 3.2 copy-done.1
  195.8 9.0 fusion.48
  206.2 3.6 multiply_reduce_fusion.4
  213.0 9.1 fusion.99
  222.1 4.1 all-gather.14.cloned.1.call-done
  226.1 9.1 fusion.98
  235.2 37.1 %all-gather.18.cloned.1.call-done = bf16[2048,768]{1,0:T(8,128)(2,1)} async-done(((bf16[128,768]{1,0:T(8,128)(2,1)}), bf16[2048,768]{1,0:T(8,128)(2,1)}) %all-gather.18.cloned.1.call-update) | async-done | bytes 3145744 | tf_op jit(solution)/shard_map/all_gather | solution.py:133
  272.3 14.4 %multiply_convert_fusion.2 = (bf16[1024,2048]{1,0:T(8,128)(2,1)S(1)}, bf16[1024,2048]{1,0:T(8,128)(2,1)}, bf16[1024,2048]{1,0:T(8,128)(2,1)}) fusion(f32[1024,2048]{1,0:T(8,128)} %fusion.98, f32[1024,2048]{1,0:T(8,128)} %fusion.99, bf16[2048,768]{1,0:T(8,128)(2,1)} %all-gather.18.cloned.1.call-done, bf16[1,1024,768]{2,1,0:T(8,128)(2,1)} %param.23), kind=kOutput, calls=%fused_computation.25 | convolution fusion | flops 3254779904 | bytes 34078720 | tf_op jit(solution)/shard_map/dot_general | solution.py:86
  286.7 7.4 fusion.100
  294.2 4.6 multiply_reduce_fusion.2
  301.7 11.9 %fusion.4 = f32[12,64,1024]{2,1,0:T(8,128)S(1)} fusion(f32[12,512]{1,0:T(8,128)S(1)} %copy-done.34, f32[12,512,1024]{2,1,0:T(8,128)} %get-tuple-element.74, pred[512,1024]{1,0:T(8,128)(4,1)S(1)} %get-tuple-element.66, bf16[1,1024,12,64]{1,3,2,0:T(8,128)(2,1)S(1)} %bitcast.217), kind=kOutput, calls=%fused_computation.17 | convolution fusion | flops 830472192 | bytes 29655040 | tf_op jit(solution)/shard_map/bhqk,bqhd->bkhd/dot_general | solution.py:217
  313.7 11.9 %add_convert_fusion = bf16[12,64,1024]{2,1,0:T(8,128)(2,1)S(1)} fusion(f32[12,64,1024]{2,1,0:T(8,128)S(1)} %fusion.4, f32[12,512]{1,0:T(8,128)S(1)} %log_add_fusion.1, f32[12,512,1024]{2,1,0:T(8,128)} %get-tuple-element.76, pred[512,1024]{1,0:T(8,128)(4,1)S(1)} %get-tuple-element.65, bf16[1,1024,12,64]{1,3,2,0:T(8,128)(2,1)S(1)} %bitcast.218), kind=kOutput, calls=%fused_computation.51 | convolution fusion | flops 832045056 | bytes 31227904 | tf_op jit(solution)/shard_map/bhqk,bqhd->bkhd/dot_general | solution.py:217
  326.7 3.0 fusion.41
  329.7 5.2 fusion.55
  334.9 18.3 %multiply_reduce_fusion = (f32[12,512]{1,0:T(8,128)S(1)}, f32[12,512,1024]{2,1,0:T(8,128)}) fusion(f32[12,512]{1,0:T(8,128)S(1)} %copy-done.34, f32[12,512,1024]{2,1,0:T(8,128)} %get-tuple-element.74, pred[512,1024]{1,0:T(8,128)(4,1)S(1)} %get-tuple-element.66, bf16[1024,12,64]{0,2,1:T(8,128)(2,1)} %convolution_convert_fusion, ...), kind=kOutput, calls=%fused_computation.2 | convolution fusion | flops 836757504 | bytes 53264384 | tf_op jit(solution)/shard_map/bqhd,bkhd->bhqk/dot_general | solution.py:220
  353.2 18.2 %multiply_reduce_fusion.1 = (f32[12,512]{1,0:T(8,128)S(1)}, f32[12,512,1024]{2,1,0:T(8,128)}) fusion(f32[12,512]{1,0:T(8,128)S(1)} %log_add_fusion.1, f32[12,512,1024]{2,1,0:T(8,128)} %get-tuple-element.76, pred[512,1024]{1,0:T(8,128)(4,1)S(1)} %get-tuple-element.65, bf16[1024,12,64]{0,2,1:T(8,128)(2,1)} %convolution_convert_fusion, ...), kind=kOutput, calls=%fused_computation.5 | convolution fusion | flops 836757504 | bytes 53264384 | tf_op jit(solution)/shard_map/bqhd,bkhd->bhqk/dot_general | solution.py:220
  371.6 42.8 %multiply_convert_fusion = (bf16[12,512,1024]{2,1,0:T(8,128)(2,1)}, bf16[12,512,1024]{2,1,0:T(8,128)(2,1)}) fusion(f32[12,512,1024]{2,1,0:T(8,128)} %get-tuple-element.83, f32[12,512]{1,0:T(8,128)S(1)} %get-tuple-element.82, f32[12,512]{1,0:T(8,128)S(1)} %copy-done.34, f32[12,512,1024]{2,1,0:T(8,128)} %get-tuple-element.74, ...), kind=kLoop, calls=%fused_computation.1 | loop fusion | flops 75497472 | bytes 126976000 | tf_op jit(solution)/shard_map/convert_element_type | solution.py:225
  414.4 7.4 fusion.87
  421.8 8.5 multiply_bitcast_fusion.2
  430.3 9.7 %multiply_bitcast_fusion.1 = f32[1,512,12,64]{1,3,2,0:T(8,128)} fusion(bf16[12,512,1024]{2,1,0:T(8,128)(2,1)} %get-tuple-element.85, bf16[1024,12,32]{0,2,1:T(8,128)(2,1)S(1)} %copy-done.12, bf16[1024,12,32]{0,2,1:T(8,128)(2,1)S(1)} %copy-done.10), kind=kOutput, calls=%fused_computation.89 | convolution fusion | flops 808845312 | bytes 15728640 | tf_op jit(solution)/shard_map/bhqk,bkhd->bqhd/dot_general | solution.py:227
  439.9 7.2 multiply_bitcast_fusion
  447.2 2.3 multiply_add_fusion.1
  450.9 2.9 fusion.43
  455.1 2.9 fusion.39
  458.1 7.5 fusion.102
  465.7 7.5 fusion.101
  474.7 8.4 fusion.32
  484.0 8.9 fusion.45
  492.9 2.8 copy.53
  495.7 4.3 fusion.103
  500.0 3.3 fusion.104
  503.6 3.5 fusion.25
  507.1 32.1 %all-reduce.4 = (bf16[768]{0:T(1024)(128)(2,1)S(1)}, bf16[768]{0:T(1024)(128)(2,1)S(1)}) all-reduce(f32[768]{0:T(1024)S(1)} %get-tuple-element.35, f32[768]{0:T(1024)S(1)} %copy-done.40), channel_id=2, replica_groups=mesh['rep'=2,'shard'=16] {'shard'}, use_global_device_ids=true, to_apply=%region_11.12.clone | all-reduce | flops 1536 | bytes 9216
  544.0 51.2 %reduce-scatter.10.cloned.1.call-done = f32[48,768]{1,0:T(8,128)} async-done(((f32[768,768]{1,0:T(8,128)}), f32[48,768]{1,0:T(8,128)}) %reduce-scatter.10.cloned.1.call-update) | async-done | bytes 147472 | tf_op jit(solution)/shard_map/reduce_scatter | solution.py:266
  596.8 86.5 %reduce-scatter.18.cloned.1.call-done = f32[48,2048]{1,0:T(8,128)} async-done(((f32[768,2048]{1,0:T(8,128)}), f32[48,2048]{1,0:T(8,128)}) %reduce-scatter.18.cloned.1.call-update) | async-done | bytes 393232 | tf_op jit(solution)/shard_map/reduce_scatter | solution.py:271
  685.0 87.4 %reduce-scatter.16.cloned.1.call-done = f32[48,2048]{1,0:T(8,128)} async-done(((f32[768,2048]{1,0:T(8,128)}), f32[48,2048]{1,0:T(8,128)}) %reduce-scatter.16.cloned.1.call-update) | async-done | bytes 393232 | tf_op jit(solution)/shard_map/reduce_scatter | solution.py:270
  774.1 86.5 %reduce-scatter.20.cloned.1.call-done = f32[128,768]{1,0:T(8,128)} async-done(((f32[2048,768]{1,0:T(8,128)}), f32[128,768]{1,0:T(8,128)}) %reduce-scatter.20.cloned.1.call-update) | async-done | bytes 393232 | tf_op jit(solution)/shard_map/reduce_scatter | solution.py:272
  862.3 5.2 fusion.24
  867.5 3.7 copy.54
  871.2 5.0 all-reduce.6
  877.2 24.1 %all-reduce.10.cloned.1.call-done = (bf16[48,768]{1,0:T(8,128)(2,1)}, bf16[48,768]{1,0:T(8,128)(2,1)}, bf16[48,768]{1,0:T(8,128)(2,1)}, bf16[48,768]{1,0:T(8,128...) async-done(((bf16[48,768]{1,0:T(8,128)(2,1)}, bf16[48,768]{1,0:T(8,128)(2,1)}, bf16[48,768]{1,0:T(8,128)(2,1)}, ...) | async-done | bytes 884752 | tf_op jit(solution)/shard_map/psum | solution.py:276
  (219 shorter events, 69.3 us)
Async XLA Ops:
  7.2 113.2 %all-gather.8.cloned.1.call-start = ((), (), s32[]{:S(2)}) async-start(), calls=%async_computation.7 | async-start | bytes 1253376 | tf_op jit(solution)/shard_map/all_gather | solution.py:128
  7.9 114.8 %all-gather.10.cloned.1.call-start = ((), (), s32[]{:S(2)}) async-start(), calls=%async_computation.8 | async-start | bytes 1253376 | tf_op jit(solution)/shard_map/all_gather | solution.py:126
  8.7 197.6 %all-gather.12.cloned.1.call-start = ((), (), s32[]{:S(2)}) async-start(), calls=%async_computation.9 | async-start | bytes 1253376 | tf_op jit(solution)/shard_map/all_gather | solution.py:129
  9.4 203.6 %all-gather.16.cloned.1.call-start = ((), (), s32[]{:S(2)}) async-start(), calls=%async_computation.11 | async-start | bytes 3342336 | tf_op jit(solution)/shard_map/all_gather | solution.py:132
  10.0 216.2 %all-gather.14.cloned.1.call-start = ((), (), s32[]{:S(2)}) async-start(), calls=%async_computation.10 | async-start | bytes 3342336 | tf_op jit(solution)/shard_map/all_gather | solution.py:131
  10.6 261.7 %all-gather.18.cloned.1.call-start = ((), (), s32[]{:S(2)}) async-start(), calls=%async_computation.12 | async-start | bytes 3342336 | tf_op jit(solution)/shard_map/all_gather | solution.py:133
  11.1 35.9 %copy-start.41 = (u32[32]{0:T(128)S(1)}, u32[32]{0:T(128)}, u32[]{:S(2)}) copy-start(u32[32]{0:T(128)} %constant.104) | copy-start | bytes 388
  11.1 37.1 %copy-start.45 = (bf16[48]{0:T(256)(128)(2,1)S(1)}, bf16[48]{0:T(256)(128)(2,1)}, u32[]{:S(2)}) copy-start(bf16[48]{0:T(256)(128)(2,1)} %param.14) | copy-start | bytes 292
  11.2 37.4 %copy-start.46 = (bf16[48]{0:T(256)(128)(2,1)S(1)}, bf16[48]{0:T(256)(128)(2,1)}, u32[]{:S(2)}) copy-start(bf16[48]{0:T(256)(128)(2,1)} %param.19) | copy-start | bytes 292
  11.2 488.8 %all-gather.20.cloned.1.call-start = ((), (), s32[]{:S(2)}) async-start(), calls=%async_computation.13 | async-start | bytes 1253376 | tf_op jit(solution)/shard_map/all_gather | solution.py:180
  11.2 7.9 collective-permute-start
  11.7 14.0 %collective-permute-start.8 = (bf16[48,768]{1,0:T(8,128)(2,1)}, bf16[48,768]{1,0:T(8,128)(2,1)S(1)}, u32[]{:S(2)}, u32[]{:S(2)}) collective-permute-start(bf16[48,768]{1,0:T(8,128)(2,1)} %param.16), channel_id=1, source_target_pairs={{1,0},{2,1},{3,2},{4,3},{5,4},{6,5},{7,6},{8,7},{9,8},{10,9},{11,1... | collective-permute-start | bytes 221192 | tf_op jit(solution)/shard_map/ppermute | solution.py:29
  16.8 522.6 %reduce-scatter.14.cloned.1.call-start = ((), (), s32[]{:S(2)}) async-start(), calls=%async_computation.17 | async-start | bytes 2506752 | tf_op jit(solution)/shard_map/reduce_scatter | solution.py:268
  19.1 6.6 collective-permute-start.1
  25.7 6.9 collective-permute-start.2
  25.7 9.8 %collective-permute-start.9 = (bf16[48,768]{1,0:T(8,128)(2,1)S(1)}, bf16[48,768]{1,0:T(8,128)(2,1)S(1)}, u32[]{:S(2)}, u32[]{:S(2)}) collective-permute-start(bf16[48,768]{1,0:T(8,128)(2,1)S(1)} %collective-permute-done.8), channel_id=1, source_target_pairs={{1,0},{2,1},{3,2},{4,3},{5,4},{6,5},{7,6},{8,7},{9,8},{10,9},{11,1... | collective-permute-start | bytes 221192 | tf_op jit(solution)/shard_map/ppermute | solution.py:29
  32.5 7.5 collective-permute-start.3
  33.7 96.9 %copy-start.28 = (f32[1024,32]{0,1:T(8,128)}, f32[1024,32]{0,1:T(8,128)S(1)}, u32[]{:S(2)}) copy-start(f32[1024,32]{0,1:T(8,128)S(1)} %get-tuple-element.71) | copy-start | bytes 393220
  35.5 70.0 %copy-start.35 = (bf16[48,768]{1,0:T(8,128)(2,1)S(1)}, bf16[48,768]{1,0:T(8,128)(2,1)}, u32[]{:S(2)}) copy-start(bf16[48,768]{1,0:T(8,128)(2,1)} %param.16) | copy-start | bytes 221188
  35.5 6.8 collective-permute-start.10
  40.0 6.9 collective-permute-start.4
  42.4 43.0 %collective-permute-start.11 = (bf16[48,768]{1,0:T(8,128)(2,1)S(1)}, bf16[48,768]{1,0:T(8,128)(2,1)S(1)}, u32[]{:S(2)}, u32[]{:S(2)}) collective-permute-start(bf16[48,768]{1,0:T(8,128)(2,1)S(1)} %collective-permute-done.10), channel_id=1, source_target_pairs={{1,0},{2,1},{3,2},{4,3},{5,4},{6,5},{7,6},{8,7},{9,8},{10,9},{11,1... | collective-permute-start | bytes 221192 | tf_op jit(solution)/shard_map/ppermute | solution.py:29
  47.0 38.4 %collective-permute-start.5 = (bf16[48,768]{1,0:T(8,128)(2,1)S(1)}, bf16[48,768]{1,0:T(8,128)(2,1)}, u32[]{:S(2)}, u32[]{:S(2)}) collective-permute-start(bf16[48,768]{1,0:T(8,128)(2,1)S(1)} %collective-permute-done.4), channel_id=1, source_target_pairs={{0,1},{1,2},{2,3},{3,4},{4,5},{5,6},{6,7},{7,8},{8,9},{9,10},{10,1... | collective-permute-start | bytes 221192 | tf_op jit(solution)/shard_map/ppermute | solution.py:27
  47.0 82.1 %copy-start.36 = (f32[1024]{0:T(1024)}, f32[1024]{0:T(1024)S(1)}, u32[]{:S(2)}) copy-start(f32[1024]{0:T(1024)S(1)} %add_rsqrt_fusion.1) | copy-start | bytes 12292
  82.8 46.3 %copy-start.38 = (f32[768]{0:T(1024)}, f32[768]{0:T(1024)S(1)}, u32[]{:S(2)}) copy-start(f32[768]{0:T(1024)S(1)} %convert_element_type.200) | copy-start | bytes 9220
  85.4 2.6 collective-permute-start.12
  85.4 7.2 collective-permute-start.6
  88.0 6.6 collective-permute-start.13
  92.6 7.0 collective-permute-start.7
  94.5 15.5 %collective-permute-start.14 = (bf16[48,768]{1,0:T(8,128)(2,1)S(1)}, bf16[48,768]{1,0:T(8,128)(2,1)S(1)}, u32[]{:S(2)}, u32[]{:S(2)}) collective-permute-start(bf16[48,768]{1,0:T(8,128)(2,1)S(1)} %collective-permute-done.13), channel_id=1, source_target_pairs={{1,0},{2,1},{3,2},{4,3},{5,4},{6,5},{7,6},{8,7},{9,8},{10,9},{11,1... | collective-permute-start | bytes 221192 | tf_op jit(solution)/shard_map/ppermute | solution.py:29
  125.1 4.0 copy-start.32
  132.1 10.8 %copy-start.11 = (bf16[1024,12,32]{0,2,1:T(8,128)(2,1)}, bf16[1024,12,32]{0,2,1:T(8,128)(2,1)S(1)}, u32[]{:S(2)}) copy-start(bf16[1024,12,32]{0,2,1:T(8,128)(2,1)S(1)} %get-tuple-element.58) | copy-start | bytes 2359300
  132.1 35.9 %copy-start.2 = (bf16[1,1024,12,32]{1,3,2,0:T(8,128)(2,1)}, bf16[1,1024,12,32]{1,3,2,0:T(8,128)(2,1)S(1)}, u32[]{:S(2)}) copy-start(bf16[1,1024,12,32]{1,3,2,0:T(8,128)(2,1)S(1)} %get-tuple-element.63) | copy-start | bytes 2359300
  132.1 35.9 %copy-start.4 = (bf16[1,1024,12,32]{1,3,2,0:T(8,128)(2,1)}, bf16[1,1024,12,32]{1,3,2,0:T(8,128)(2,1)S(1)}, u32[]{:S(2)}) copy-start(bf16[1,1024,12,32]{1,3,2,0:T(8,128)(2,1)S(1)} %get-tuple-element.64) | copy-start | bytes 2359300
  132.2 35.9 %copy-start.9 = (bf16[1024,12,32]{0,2,1:T(8,128)(2,1)}, bf16[1024,12,32]{0,2,1:T(8,128)(2,1)S(1)}, u32[]{:S(2)}) copy-start(bf16[1024,12,32]{0,2,1:T(8,128)(2,1)S(1)} %get-tuple-element.57) | copy-start | bytes 2359300
  142.9 15.5 %copy-start = (f32[12,512,1024]{2,1,0:T(8,128)S(1)}, f32[12,512,1024]{2,1,0:T(8,128)}, u32[]{:S(2)}) copy-start(f32[12,512,1024]{2,1,0:T(8,128)} %get-tuple-element.74) | copy-start | bytes 75497472
  180.2 15.6 %copy-start.1 = (f32[12,512,1024]{2,1,0:T(8,128)S(1)}, f32[12,512,1024]{2,1,0:T(8,128)}, u32[]{:S(2)}) copy-start(f32[12,512,1024]{2,1,0:T(8,128)} %get-tuple-element.76) | copy-start | bytes 75497472
  195.8 9.0 copy-start.33
  272.3 14.4 %copy-start.43 = (bf16[768,2048]{1,0:T(8,128)(2,1)S(1)}, bf16[768,2048]{1,0:T(8,128)(2,1)}, u32[]{:S(2)}) copy-start(bf16[768,2048]{1,0:T(8,128)(2,1)} %all-gather.14.cloned.1.call-done) | copy-start | bytes 9437188
  286.7 7.4 copy-start.47
  286.7 7.4 copy-start.7
  286.7 7.4 copy-start.42
  294.1 4.6 copy-start.13
  301.7 12.0 %copy-start.27 = (bf16[1024,768]{0,1:T(8,128)(2,1)}, bf16[1024,768]{0,1:T(8,128)(2,1)S(1)}, u32[]{:S(2)}) copy-start(bf16[1024,768]{0,1:T(8,128)(2,1)S(1)} %convolution_convert_fusion.1) | copy-start | bytes 4718596
  313.6 13.1 %copy-start.37 = (f32[1024]{0:T(1024)S(1)}, f32[1024]{0:T(1024)}, u32[]{:S(2)}) copy-start(f32[1024]{0:T(1024)} %copy-done.36) | copy-start | bytes 12292
  313.7 13.1 %copy-start.39 = (f32[768]{0:T(1024)S(1)}, f32[768]{0:T(1024)}, u32[]{:S(2)}) copy-start(f32[768]{0:T(1024)} %copy-done.38) | copy-start | bytes 9220
  334.9 206.0 %reduce-scatter.12.cloned.1.call-start = ((), (), s32[]{:S(2)}) async-start(), calls=%async_computation.16 | async-start | bytes 2506752 | tf_op jit(solution)/shard_map/reduce_scatter | solution.py:267
  371.5 171.0 %reduce-scatter.8.cloned.1.call-start = ((), (), s32[]{:S(2)}) async-start(), calls=%async_computation.14 | async-start | bytes 2506752 | tf_op jit(solution)/shard_map/reduce_scatter | solution.py:265
  371.5 42.8 %copy-start.3 = (bf16[1,1024,12,32]{1,3,2,0:T(8,128)(2,1)S(1)}, bf16[1,1024,12,32]{1,3,2,0:T(8,128)(2,1)}, u32[]{:S(2)}) copy-start(bf16[1,1024,12,32]{1,3,2,0:T(8,128)(2,1)} %copy-done.2) | copy-start | bytes 2359300
  371.5 42.8 %copy-start.5 = (bf16[1,1024,12,32]{1,3,2,0:T(8,128)(2,1)S(1)}, bf16[1,1024,12,32]{1,3,2,0:T(8,128)(2,1)}, u32[]{:S(2)}) copy-start(bf16[1,1024,12,32]{1,3,2,0:T(8,128)(2,1)} %copy-done.4) | copy-start | bytes 2359300
  414.3 7.4 copy-start.10
  414.3 7.4 copy-start.12
  439.9 7.2 copy-start.14
  439.9 7.3 copy-start.29
  439.9 7.3 copy-start.31
  453.8 141.4 %reduce-scatter.10.cloned.1.call-start = ((), (), s32[]{:S(2)}) async-start(), calls=%async_computation.15 | async-start | bytes 2506752 | tf_op jit(solution)/shard_map/reduce_scatter | solution.py:266
  458.0 225.2 %reduce-scatter.18.cloned.1.call-start = ((), (), s32[]{:S(2)}) async-start(), calls=%async_computation.19 | async-start | bytes 6684672 | tf_op jit(solution)/shard_map/reduce_scatter | solution.py:271
  465.6 306.8 %reduce-scatter.16.cloned.1.call-start = ((), (), s32[]{:S(2)}) async-start(), calls=%async_computation.18 | async-start | bytes 6684672 | tf_op jit(solution)/shard_map/reduce_scatter | solution.py:270
  473.2 387.3 %reduce-scatter.20.cloned.1.call-start = ((), (), s32[]{:S(2)}) async-start(), calls=%async_computation.20 | async-start | bytes 6684672 | tf_op jit(solution)/shard_map/reduce_scatter | solution.py:272
  483.1 418.2 %all-reduce.10.cloned.1.call-start = ((), (), s32[]{:S(2)}) async-start(), calls=%async_computation.21 | async-start | bytes 1769472 | tf_op jit(solution)/shard_map/psum | solution.py:276
  484.0 11.7 %copy-start.22 = (bf16[1,1024,12,64]{1,3,2,0:T(8,128)(2,1)S(1)}, bf16[1,1024,12,64]{1,3,2,0:T(8,128)(2,1)}, u32[]{:S(2)}) copy-start(bf16[1,1024,12,64]{1,3,2,0:T(8,128)(2,1)} %copy-done.21) | copy-start | bytes 4718596
  500.0 3.3 copy-start.19
  500.0 3.6 copy-start.26
  503.6 3.5 copy-start.40
  (14 other events, 27.2 us)
Sparse Core Ops, SparseCore 0:
  10.3 42.7 all-gather.7
  55.3 38.4 all-gather.9
  96.1 37.4 all-gather.11
  135.8 44.1 all-gather.15
  182.1 43.9 all-gather.13
  228.3 43.9 all-gather.17
  274.6 37.1 all-gather.19
  335.0 61.8 reduce-scatter.13
  401.1 61.9 reduce-scatter.11
  466.7 62.0 reduce-scatter.7
  533.0 62.1 reduce-scatter.9
  599.0 84.2 reduce-scatter.17
  687.7 84.6 reduce-scatter.15
  776.2 84.3 reduce-scatter.19
  864.5 36.7 all-reduce.9
